TPU v7x, 32 devices: a whole 2x2x4 slice. The times are simulated.
32 devices in a mesh: lat: 8 (over y, x, core), lev: 4 (over z).
Axes of the slice: x: 2, y: 2, z: 4, core: 2. Of those that a mesh axis runs over, the one named last changes fastest.
Arguments:
- tracer: float32 [8, 640, 1280], P('lev', 'lat'), may hold values from -6 to 6
- offsets: int32 [2, 640, 1280], P(None, 'lat'), may hold values from -3 to 3
- stencil: float32 [7, 7], replicated, may hold values from -0.6 to 0.6
- assign: int32 [640], replicated, may hold values from 0 to 639, as said below
- legendre: bfloat16 [640, 2, 320, 320], P('lat', None, 'lev'), may hold values from -0.3125 to 0.3125
- damping: float32 [8], replicated, may hold values from 0.5 to 8
- vert_vecs: float32 [8, 8], replicated, may hold values from -2 to 2
- vert_inv: float32 [8, 8], replicated, may hold values from -2 to 2
Outputs:
- tracer_new: float32 [8, 640, 1280], P('lev', 'lat')
- spectral_new: float32 [640, 2, 320, 16], P('lat', None, 'lev')
Inputs may be any that keep to these rules, and one draw needn't show every extreme that they name: `assign`: a permutation of 0 to 639 in which slots 2 u and 2 u + 1 hold the wavenumbers m and 639 - m.
All inputs are finite; a program needn't handle non-finite values.
Results may differ from a plain program's by a relative error of at most 0.0036.
Values may be sent and summed in bfloat16 or wider, within the bound.
A program may use at most 192 MiB of HBM per device.

v0:
```python
import math
import jax
import jax.numpy as jnp
from jax import lax
from jax.sharding import PartitionSpec as P

M = 640
EXACT = lax.Precision.HIGHEST


def padded_2(cells, sides, width):
    for axis, dim in sides:
        count = lax.axis_size(axis)
        ends = count - 1
        head = lax.slice_in_dim(cells, 0, width, axis=dim)
        tail = lax.slice_in_dim(cells, cells.shape[dim] - width, cells.shape[dim], axis=dim)
        cells = jnp.concatenate(
            [
                lax.ppermute(tail, axis, [(i, (i + 1) % count) for i in range(ends)]),
                cells,
                lax.ppermute(head, axis, [((i + 1) % count, i) for i in range(ends)]),
            ],
            axis=dim,
        )
    return cells


def transport(padded, offsets, stencil):
    row_count = offsets.shape[1]
    summed = jnp.zeros((padded.shape[0], row_count, padded.shape[2]), jnp.float32)
    for row_step in range(-3, 4):
        band_rows = padded[:, 3 + row_step : 3 + row_step + row_count, :]
        for col_step in range(-3, 4):
            shifted = jnp.roll(band_rows, -col_step, axis=2)
            picked = jnp.logical_and(offsets[0] == row_step, offsets[1] == col_step).astype(
                jnp.float32
            )
            summed = summed + (stencil[row_step + 3, col_step + 3] + picked)[None, :, :] * shifted
    return summed


def wave_angles(assign, lon_cells):
    longitudes = jnp.arange(lon_cells, dtype=jnp.int32)
    phase_index = longitudes[:, None] * assign[None, :] % lon_cells
    angles = phase_index.astype(jnp.float32) * (2.0 * math.pi / lon_cells)
    return (angles, 1.0 / math.sqrt(lon_cells))


def forward_table(assign, lon_cells):
    angles, norm_scale = wave_angles(assign, lon_cells)
    return jnp.stack([jnp.cos(angles) * norm_scale, -jnp.sin(angles) * norm_scale], axis=2)


def inverse_table(assign, lon_cells):
    angles, norm_scale = wave_angles(assign, lon_cells)
    weights = jnp.where(assign == 0, 1.0, 2.0).astype(jnp.float32) * norm_scale
    cosines = jnp.cos(angles).T * weights[:, None]
    sines = -jnp.sin(angles).T * weights[:, None]
    return jnp.stack([cosines, sines], axis=1)


def split_hemispheres(fourier):
    half_lat = fourier.shape[-1] // 2
    north_half = fourier[..., :half_lat]
    south_half = fourier[..., ::-1][..., :half_lat]
    return jnp.stack([north_half + south_half, north_half - south_half], axis=1).astype(
        jnp.bfloat16
    )


def vertical(spectra, my_waves, first_degree, damping, vert_vecs, vert_inv):
    degree_span = spectra.shape[2]
    degrees = first_degree + jnp.arange(degree_span, dtype=jnp.int32)
    parity = jnp.arange(2, dtype=jnp.int32)
    degree_n = my_waves[:, None, None] + 2 * degrees[None, None, :] + parity[None, :, None]
    inside = (degree_n <= M - 1).astype(jnp.float32)
    forcing = spectra * inside[:, :, :, None, None]
    modal = jnp.einsum("kq,rpicq->rpick", vert_inv, forcing, precision=EXACT)
    scaled_n = degree_n.astype(jnp.float32)
    growth = scaled_n * (scaled_n + 1.0) / float(M * M)
    denominator = 1.0 + growth[:, :, :, None, None] * damping[None, None, None, None, :]
    modal = modal / denominator
    return jnp.einsum("kq,rpicq->rpick", vert_vecs, modal, precision=EXACT)


def on_device(tracer, offsets, stencil, assign, legendre, damping, vert_vecs, vert_inv):
    lon_cells = tracer.shape[2]
    padded = padded_2(tracer, (("lat", 1),), 3)
    advected = transport(padded, offsets, stencil)
    fourier = jnp.einsum(
        "lij,jrc->rcli", advected, forward_table(assign, lon_cells), precision=EXACT
    )
    by_wave = lax.all_to_all(fourier, "lat", split_axis=0, concat_axis=3, tiled=True)
    hemispheres = split_hemispheres(by_wave)
    slot_count = legendre.shape[0]
    my_waves = lax.dynamic_slice_in_dim(assign, lax.axis_index("lat") * slot_count, slot_count)
    first_degree = lax.axis_index("lev") * legendre.shape[2]
    full_table = lax.all_gather(legendre, "lev", axis=2, tiled=True)
    spectra_all = jnp.einsum(
        "rpij,rpclj->rpicl", full_table, hemispheres, preferred_element_type=jnp.float32
    )
    spectra = lax.all_to_all(spectra_all, "lev", split_axis=2, concat_axis=4, tiled=True)
    solved = vertical(spectra, my_waves, first_degree, damping, vert_vecs, vert_inv)
    packed = solved.astype(jnp.bfloat16)
    spread = lax.all_to_all(packed, "lev", split_axis=4, concat_axis=2, tiled=True)
    back_terms = jnp.einsum(
        "rpij,rpicl->lrpcj", full_table, spread, preferred_element_type=jnp.float32
    )
    north_half = back_terms[:, :, 0] + back_terms[:, :, 1]
    south_half = back_terms[:, :, 0] - back_terms[:, :, 1]
    zonal = jnp.concatenate([north_half, south_half[..., ::-1]], axis=-1)
    lat_rows = lax.all_to_all(zonal, "lat", split_axis=3, concat_axis=1, tiled=True)
    tracer_new = jnp.einsum(
        "lrci,rcj->lij", lat_rows, inverse_table(assign, lon_cells), precision=EXACT
    )
    spectral_new = solved.reshape(solved.shape[0], 2, solved.shape[2], 2 * solved.shape[4])
    return (tracer_new, spectral_new)


def solution(mesh):
    in_specs = (
        P("lev", "lat", None),
        P(None, "lat", None),
        P(),
        P(),
        P("lat", None, "lev", None),
        P(),
        P(),
        P(),
    )
    out_specs = (P("lev", "lat", None), P("lat", None, "lev", None))
    return jax.shard_map(
        on_device, mesh=mesh, in_specs=in_specs, out_specs=out_specs, check_vma=False
    )
```

profile of v0, /device:TPU:0, one launch (start us, length us, event | category | flops | bytes accessed | tf_op | source)
XLA Modules:
  0.0 811.9 jit_solution(14464015490012806624)
XLA Ops:
  15.8 5.6 add_bitcast_fusion.41
  21.4 5.5 add_bitcast_fusion.47
  28.3 9.1 %add_bitcast_fusion.26 = (f32[80,1280]{1,0:T(8,128)}, f32[80,1280]{1,0:T(8,128)}, f32[80,1280]{1,0:T(8,128)}, f32[80,1280]{1,0:T(8,128)}, f32[80,1280]{1,0:T(8,1...) fusion(pred[1,80,1280]{2,1,0:T(8,128)(4,1)S(1)} %get-tuple-elem, ...), kind=kLoop, calls=%fused_computation.329 | loop fusion | flops 3379200 | bytes 5324844 | tf_op jit(solution)/shard_map/mul | solution.py:38
  37.4 9.3 %add_bitcast_fusion.40 = (f32[80,1280]{1,0:T(8,128)S(1)}, f32[80,1280]{1,0:T(8,128)S(1)}, f32[80,1280]{1,0:T(8,128)S(1)}, f32[80,1280]{1,0:T(8,128)S(1)}, f32[80...) fusion(pred[1,80,1280]{2,1,0:T(8,128)(4,1)S(1)} %get-tuple-elem, ...), kind=kLoop, calls=%fused_computation.357 | loop fusion | flops 3686400 | bytes 5632048 | tf_op jit(solution)/shard_map/mul | solution.py:38
  46.6 9.6 %add_bitcast_fusion.38 = (f32[80,1280]{1,0:T(8,128)}, f32[80,1280]{1,0:T(8,128)}, f32[80,1280]{1,0:T(8,128)}, f32[80,1280]{1,0:T(8,128)}, f32[80,1280]{1,0:T(8,1...) fusion(pred[1,80,1280]{2,1,0:T(8,128)(4,1)S(1)} %get-tuple-elem, ...), kind=kLoop, calls=%fused_computation.353 | loop fusion | flops 3686400 | bytes 5632048 | tf_op jit(solution)/shard_map/mul | solution.py:38
  56.2 23.1 %cosine_multiply_fusion.1 = (f32[1280,640,1]{1,0,2:T(8,128)S(1)}, f32[1280,640,1]{1,0,2:T(8,128)S(1)}) fusion(s32[640]{0:T(1024)S(1)} %copy-done.5), kind=kLoop, calls=%fused_computation.62 | loop fusion | flops 9830400 | bytes 6556160 | tf_op jit(solution)/shard_map/mul | solution.py:51
  84.8 2.9 fusion.231
  87.8 2.9 fusion.233
  90.7 3.0 fusion.235
  93.7 3.8 fusion.72
  97.5 3.8 fusion.73
  101.3 3.7 fusion.237
  105.0 28.9 %fusion.4 = f32[640,2,2,80]{0,3,2,1:T(8,128)S(1)} fusion(f32[1280,640,1]{1,0,2:T(8,128)S(1)} %get-tuple-element.229, f32[1280,640,1]{1,0,2:T(8,128)S(1)} %get-tuple-element.228, f32[2,83,1280]{2,1,0:T(8,128)S(1)} %constant_dynamic-update-slice_fusion, f32[2,80,1]{2,1,0:T(8,128)} %get-tuple-element.138, f32[2,80,1279]{2,1,0:T(8,128)} %get-tuple-element.137, ...), kind=kOutput, calls=%fused_computation.43 | convolution fusion | flops 3176652800 | bytes 65405440 | tf_op jit(solution)/shard_map/lij,jrc->rcli/dot_general | solution.py:90
  134.8 25.3 %all_to_all.72 = f32[640,2,2,80]{3,2,1,0:T(2,128)S(1)} all-to-all(f32[640,2,2,80]{3,2,1,0:T(2,128)S(1)} %copy.54), channel_id=1, replica_groups=mesh['lat'=8,'lev'=4] {'lat'}, dimensions={0} | all-to-all | bytes 1638400 | tf_op jit(solution)/shard_map/all_to_all | solution.py:93
  164.9 504.5 %all-gather.2.cloned.1.call-done = bf16[80,2,320,320]{3,2,1,0:T(8,128)(2,1)} async-done(((bf16[80,2,80,320]{3,2,1,0:T(8,128)(2,1)}), bf16[80,2,320,320]{3,2,1,0:T(8,128)(2,1)}) %all-gather.2.cloned.1.call-update) | async-done | bytes 32768016 | tf_op jit(solution)/shard_map/all_gather | solution.py:98
  669.5 17.4 %fusion.21 = f32[80,2,320,2,2]{2,4,3,1,0:T(2,128)S(1)} fusion(bf16[80,2,320,320]{3,2,1,0:T(8,128)(2,1)} %all-gather.2.cloned.1.call-done, bf16[80,1,2,2,320]{4,3,2,1,0:T(2,128)(2,1)S(1)} %fusion.204, bf16[80,1,2,2,320]{4,3,2,1,0:T(2,128)(2,1)S(1)} %get-tuple-element.2), kind=kOutput, calls=%fused_computation.70 | convolution fusion | flops 131891200 | bytes 33996800 | tf_op jit(solution)/shard_map/rpij,rpclj->rpicl/dot_general | solution.py:99
  689.0 3.5 all-to-all-start.1
  693.7 30.4 %all-to-all-done.1 = f32[80,2,320,2,2]{0,4,3,1,2:T(2,128)S(1)} async-done(((f32[80,2,320,2,2]{0,4,3,1,2:T(2,128)}), f32[80,2,320,2,2]{0,4,3,1,2:T(2,128)S(1)}, u32[]{:S(2)}, u32[]{:S(2)}) %all-to-all-start.1) | async-done | bytes 819232 | tf_op jit(solution)/shard_map/all_to_all | solution.py:102
  730.8 19.7 %all_to_all.73 = bf16[80,2,80,2,8]{2,3,1,0,4:T(2,128)(2,1)S(1)} all-to-all(bf16[80,2,80,2,8]{2,3,1,0,4:T(2,128)(2,1)S(1)} %copy.62), channel_id=1, replica_groups=mesh['lat'=8,'lev'=4] {'lev'}, dimensions={4} | all-to-all | bytes 819200 | tf_op jit(solution)/shard_map/all_to_all | solution.py:105
  752.6 15.5 %fusion.24 = f32[2,80,2,2,320]{4,0,3,2,1:T(2,128)S(1)} fusion(bf16[80,2,320,2,2]{2,4,3,1,0:T(2,128)(2,1)S(1)} %all_to_all.63, bf16[80,2,320,320]{3,2,1,0:T(8,128)(2,1)} %all-gather.2.cloned.1.call-done), kind=kOutput, calls=%fused_computation.71 | convolution fusion | flops 131072000 | bytes 33996800 | tf_op jit(solution)/shard_map/rpij,rpicl->lrpcj/dot_general | solution.py:106
  771.3 2.7 copy.67
  774.1 3.8 all-to-all-start.3
  777.9 16.0 %cosine_multiply_fusion = (f32[640,1,1280]{2,0,1:T(8,128)}, f32[640,1,1280]{2,0,1:T(8,128)}) fusion(f32[640]{0:T(1024)S(1)} %select_multiply_fusion, s32[640]{0:T(1024)S(1)} %copy-done.5), kind=kLoop, calls=%fused_computation.57 | loop fusion | flops 9830400 | bytes 6558720 | tf_op jit(solution)/shard_map/mul | solution.py:57
  797.2 7.7 fusion.20
  (68 shorter events, 39.5 us)
Async XLA Ops:
  7.2 720.9 %copy-start = (f32[8,8]{1,0:T(8,128)S(1)}, f32[8,8]{1,0:T(8,128)}, u32[]{:S(2)}) copy-start(f32[8,8]{1,0:T(8,128)} %param.14) | copy-start | bytes 772
  7.2 1.2 copy-start.1
  7.2 4.9 copy-start.4
  7.2 7.0 copy-start.2
  7.2 662.3 %all-gather.2.cloned.1.call-start = ((), (), s32[]{:S(2)}) async-start(), calls=%async_computation.4 | async-start | bytes 49152000 | tf_op jit(solution)/shard_map/all_gather | solution.py:98
  8.4 73.7 %collective-permute-start = (f32[2,3,1280]{2,1,0:T(4,128)S(1)}, f32[2,3,1280]{2,1,0:T(4,128)S(1)}, u32[]{:S(2)}, u32[]{:S(2)}) collective-permute-start(f32[2,3,1280]{2,1,0:T(4,128)S(1)} %get-tuple-element.140), channel_id=1, source_target_pairs={{0,4},{4,8},{8,12},{12,16},{16,20},{20,24},{24,28},{1,5},{5,9},{9,... | collective-permute-start | bytes 92168 | tf_op jit(solution)/shard_map/ppermute | solution.py:19
  10.8 68.7 %collective-permute-start.1 = (f32[2,3,1280]{2,1,0:T(4,128)S(1)}, f32[2,3,1280]{2,1,0:T(4,128)S(1)}, u32[]{:S(2)}, u32[]{:S(2)}) collective-permute-start(f32[2,3,1280]{2,1,0:T(4,128)S(1)} %get-tuple-element.141), channel_id=1, source_target_pairs={{4,0},{8,4},{12,8},{16,12},{20,16},{24,20},{28,24},{5,1},{9,5},{13... | collective-permute-start | bytes 92168 | tf_op jit(solution)/shard_map/ppermute | solution.py:21
  46.6 9.6 %copy-start.5 = (s32[640]{0:T(1024)S(1)}, s32[640]{0:T(1024)}, u32[]{:S(2)}) copy-start(s32[640]{0:T(1024)} %param.11) | copy-start | bytes 7684
  686.9 5.9 copy-start.6
  689.0 35.2 %all-to-all-start.1 = ((f32[80,2,320,2,2]{0,4,3,1,2:T(2,128)}), f32[80,2,320,2,2]{0,4,3,1,2:T(2,128)S(1)}, u32[]{:S(2)}, u32[]{:S(2)}) async-start(f32[80,2,320,2,2]{0,4,3,1,2:T(2,128)} %copy.57), calls=%async_computation.1 | async-start | bytes 2621440 | tf_op jit(solution)/shard_map/all_to_all | solution.py:102
  725.3 1.1 copy-start.3
  725.3 1.1 copy-start.7
  774.1 21.9 %all-to-all-start.3 = ((f32[2,80,2,640]{1,2,0,3:T(2,128)}), f32[2,80,2,640]{1,2,0,3:T(2,128)S(1)}, u32[]{:S(2)}, u32[]{:S(2)}) async-start(f32[2,80,2,640]{1,2,0,3:T(2,128)} %copy.67), calls=%async_computation.3 | async-start | bytes 2621440 | tf_op jit(solution)/shard_map/all_to_all | solution.py:112
Sparse Core Ops, SparseCore 0:
  9.6 659.8 all-gather.1
where the time goes:
time: 821 us; the launch traced here: 812 us
  waiting for transfers between devices  538 us (66%)
  other arithmetic  98.4 us (12%)
  matrix products  73.4 us (9%)
  blocking collectives  45 us (5%)
  local copies, waits for them, and re-layouts  31.8 us (4%)
  between operations  14.6 us (2%)
  starting transfers between devices  11.1 us (1%)
    all_gather x1, waiting for transfers between devices, on_device(): full_table = lax.all_gather(legendre, 'lev', axis=2, tiled=True)  505 us
    mul x7, other arithmetic, transport(): (stencil[row_step + 3, col_step + 3] + picked)[None, :, :] * shifted  42 us
    all_to_all x1, waiting for transfers between devices, on_device(): lax.all_to_all(spectra_all, 'lev', split_axis=2, concat_axis=4, tiled=True)  30.4 us
    dot_general x1, matrix products, on_device(): jnp.einsum('lij,jrc->rcli', advected, forward_table(assign, lon_cells), p...  28.9 us
    all_to_all x1, blocking collectives, on_device(): lax.all_to_all(fourier, 'lat', split_axis=0, concat_axis=3, tiled=True)  25.3 us
    mul x1, other arithmetic, forward_table(): jnp.cos(angles) * norm_scale  23.1 us
    all_to_all x1, blocking collectives, on_device(): lax.all_to_all(packed, 'lev', split_axis=4, concat_axis=2, tiled=True)  19.7 us
    dot_general x1, matrix products, on_device(): jnp.einsum('rpij,rpclj->rpicl', full_table, hemispheres, preferred_elemen...  17.4 us
  transfers between devices with their start and end apart: 5, of which 3 were waited for; matrix products, arithmetic and copies ran while one was open for 18% of the time, Pallas kernels for 0%

commit v1 on v0

--- a/solution.py
+++ b/solution.py
@@ -95,7 +95,12 @@
     slot_count = legendre.shape[0]
     my_waves = lax.dynamic_slice_in_dim(assign, lax.axis_index("lat") * slot_count, slot_count)
     first_degree = lax.axis_index("lev") * legendre.shape[2]
-    full_table = lax.all_gather(legendre, "lev", axis=2, tiled=True)
+    ring = [legendre]
+    for hop in range(3):
+        ring.append(lax.ppermute(ring[-1], "lev", [(dev, (dev + 1) % 4) for dev in range(4)]))
+    full_table = jnp.roll(
+        jnp.concatenate(ring[::-1], axis=2), (lax.axis_index("lev") + 1) * ring[0].shape[2], axis=2
+    )
     spectra_all = jnp.einsum(
         "rpij,rpclj->rpicl", full_table, hemispheres, preferred_element_type=jnp.float32
     )

time: 821 us -> 859 us (1.046)
  local copies, waits for them, and re-layouts: 31.8 us -> 105 us
  blocking collectives: 45 us -> 19.5 us
  between operations: 14.6 us -> 1.52 us
    all_gather x1 -> x0, waiting for transfers between devices: 505 us -> none  [on_device(): full_table = lax.all_gather(legendre, 'lev', axis=2, tiled=True)]
    ppermute x0 -> x3, waiting for transfers between devices: none -> 490 us  [on_device(): lax.ppermute(ring[-1], 'lev', [(dev, (dev + 1) % 4) for dev in range(4)])]
    unnamed x20 -> x27, local copies, waits for them, and re-layouts: 4.81 us -> 64.1 us
    all_to_all x1 -> x0, blocking collectives: 25.3 us -> none  [on_device(): lax.all_to_all(fourier, 'lat', split_axis=0, concat_axis=3, tiled=True)]
    all_to_all x0 -> x1, waiting for transfers between devices: none -> 18.1 us  [on_device(): lax.all_to_all(fourier, 'lat', split_axis=0, concat_axis=3, tiled=True)]
    mul x1, other arithmetic: 23.1 us -> 13.4 us  [forward_table(): jnp.cos(angles) * norm_scale]
  transfers between devices with their start and end apart: 5 -> 8, of which waited for: 3 -> 6; matrix products, arithmetic and copies ran while one was open for 18% -> 17% of each run, Pallas kernels for 0% -> 0%
where the time goes in v1:
time: 859 us; the launch traced here: 849 us
  waiting for transfers between devices  538 us (63%)
  local copies, waits for them, and re-layouts  105 us (12%)
  other arithmetic  90.7 us (11%)
  matrix products  74.5 us (9%)
  blocking collectives  19.5 us (2%)
  starting transfers between devices  18.9 us (2%)
    ppermute x3, waiting for transfers between devices, on_device(): lax.ppermute(ring[-1], 'lev', [(dev, (dev + 1) % 4) for dev in range(4)])  490 us
    unnamed x27, local copies, waits for them, and re-layouts  64.1 us
    mul x7, other arithmetic, transport(): (stencil[row_step + 3, col_step + 3] + picked)[None, :, :] * shifted  44 us
    dot_general x1, matrix products, on_device(): jnp.einsum('lij,jrc->rcli', advected, forward_table(assign, lon_cells), p...  28.9 us
    all_to_all x1, waiting for transfers between devices, on_device(): lax.all_to_all(spectra_all, 'lev', split_axis=2, concat_axis=4, tiled=True)  28.1 us
    all_to_all x1, blocking collectives, on_device(): lax.all_to_all(packed, 'lev', split_axis=4, concat_axis=2, tiled=True)  19.5 us
    all_to_all x1, waiting for transfers between devices, on_device(): lax.all_to_all(fourier, 'lat', split_axis=0, concat_axis=3, tiled=True)  18.1 us
    dot_general x1, matrix products, on_device(): jnp.einsum('rpij,rpclj->rpicl', full_table, hemispheres, preferred_elemen...  17.4 us
  transfers between devices with their start and end apart: 8, of which 6 were waited for; matrix products, arithmetic and copies ran while one was open for 17% of the time, Pallas kernels for 0%

profile of v1, /device:TPU:0, one launch (start us, length us, event | category | flops | bytes accessed | tf_op | source)
XLA Modules:
  0.0 848.7 jit_solution(1253650065297277753)
XLA Ops:
  3.8 213.6 %collective-permute-done = bf16[80,2,80,320]{3,2,1,0:T(8,128)(2,1)S(1)} collective-permute-done((bf16[80,2,80,320]{3,2,1,0:T(8,128)(2,1)}, bf16[80,2,80,320]{3,2,1,0:T(8,128)(2,1)S(1)}, u32[]{:S(2)}, u32[]{:S(2)}) %collective-permute-start) | collective-permute-done | bytes 8192032 | tf_op jit(solution)/shard_map/ppermute | solution.py:100
  231.5 6.5 add_bitcast_fusion.41
  245.0 8.8 %add_bitcast_fusion.26 = (f32[80,1280]{1,0:T(8,128)}, f32[80,1280]{1,0:T(8,128)}, f32[80,1280]{1,0:T(8,128)}, f32[80,1280]{1,0:T(8,128)}, f32[80,1280]{1,0:T(8,1...) fusion(pred[1,80,1280]{2,1,0:T(8,128)(4,1)S(1)} %get-tuple-elem, ...), kind=kLoop, calls=%fused_computation.330 | loop fusion | flops 3379200 | bytes 5324844 | tf_op jit(solution)/shard_map/mul | solution.py:38
  253.8 9.4 %add_bitcast_fusion.38 = (f32[80,1280]{1,0:T(8,128)S(1)}, f32[80,1280]{1,0:T(8,128)S(1)}, f32[80,1280]{1,0:T(8,128)S(1)}, f32[80,1280]{1,0:T(8,128)S(1)}, f32[80...) fusion(pred[1,80,1280]{2,1,0:T(8,128)(4,1)S(1)} %get-tuple-elem, ...), kind=kLoop, calls=%fused_computation.354 | loop fusion | flops 3686400 | bytes 5632048 | tf_op jit(solution)/shard_map/mul | solution.py:38
  263.2 9.7 %add_bitcast_fusion.40 = (f32[80,1280]{1,0:T(8,128)}, f32[80,1280]{1,0:T(8,128)}, f32[80,1280]{1,0:T(8,128)}, f32[80,1280]{1,0:T(8,128)}, f32[80,1280]{1,0:T(8,1...) fusion(pred[1,80,1280]{2,1,0:T(8,128)(4,1)S(1)} %get-tuple-elem, ...), kind=kLoop, calls=%fused_computation.358 | loop fusion | flops 3686400 | bytes 5632048 | tf_op jit(solution)/shard_map/mul | solution.py:38
  272.9 13.4 %cosine_multiply_fusion.1 = (f32[1280,640,1]{1,0,2:T(8,128)S(1)}, f32[1280,640,1]{1,0,2:T(8,128)S(1)}) fusion(s32[640]{0:T(1024)S(1)} %copy-done.5), kind=kLoop, calls=%fused_computation.64 | loop fusion | flops 9830400 | bytes 6556160 | tf_op jit(solution)/shard_map/mul | solution.py:51
  289.0 142.8 %collective-permute-done.1 = bf16[80,2,80,320]{3,2,1,0:T(8,128)(2,1)} collective-permute-done((bf16[80,2,80,320]{3,2,1,0:T(8,128)(2,1)S(1)}, bf16[80,2,80,320]{3,2,1,0:T(8,128)(2,1)}, u32[]{:S(2)}, u32[]{:S(2)}) %collective-permute-start.1) | collective-permute-done | bytes 8192032 | tf_op jit(solution)/shard_map/ppermute | solution.py:100
  455.1 28.9 %fusion.6 = f32[640,2,2,80]{0,3,2,1:T(8,128)S(1)} fusion(f32[1280,640,1]{1,0,2:T(8,128)S(1)} %get-tuple-element.229, f32[1280,640,1]{1,0,2:T(8,128)S(1)} %get-tuple-element.228, f32[2,83,1280]{2,1,0:T(8,128)S(1)} %constant_dynamic-update-slice_fusion.8, f32[2,80,1]{2,1,0:T(8,128)} %get-tuple-element.138, f32[2,80,1279]{2,1,0:T(8,128)} %get-tuple-element.137, ...), kind=kOutput, calls=%fused_computation.45 | convolution fusion | flops 3176652800 | bytes 65405440 | tf_op jit(solution)/shard_map/lij,jrc->rcli/dot_general | solution.py:90
  489.2 18.1 %all-to-all-done = f32[640,2,2,80]{3,2,1,0:T(2,128)S(1)} async-done(((f32[640,2,2,80]{3,2,1,0:T(2,128)}), f32[640,2,2,80]{3,2,1,0:T(2,128)S(1)}, u32[]{:S(2)}, u32[]{:S(2)}) %all-to-all-start) | async-done | bytes 819232 | tf_op jit(solution)/shard_map/all_to_all | solution.py:93
  512.0 133.9 %collective-permute-done.2 = bf16[80,2,80,320]{3,2,1,0:T(8,128)(2,1)} collective-permute-done((bf16[80,2,80,320]{3,2,1,0:T(8,128)(2,1)}, bf16[80,2,80,320]{3,2,1,0:T(8,128)(2,1)}, u32[]{:S(2)}, u32[]{:S(2)}) %collective-permute-start.2) | collective-permute-done | bytes 8192032 | tf_op jit(solution)/shard_map/ppermute | solution.py:100
  645.9 8.5 %constant_dynamic-update-slice_fusion.7 = bf16[80,2,640,320]{3,2,1,0:T(8,128)(2,1)} fusion(bf16[80,2,80,320]{3,2,1,0:T(8,128)(2,1)} %collective-permute-done.2), kind=kLoop, calls=%fused_computation.420 | loop fusion | bytes 18022400
  654.4 8.6 %constant_dynamic-update-slice_fusion.6 = bf16[80,2,640,320]{3,2,1,0:T(8,128)(2,1)} fusion(bf16[80,2,640,320]{3,2,1,0:T(8,128)(2,1)} %constant_dynamic-update-slice_fusion.7, bf16[80,2,80,320]{3,2,1,0:T(8,128)(2,1)} %collective-permute-done.1), kind=kLoop, calls=%fused_computation.419 | loop fusion | bytes 19660800
  663.0 8.5 %constant_dynamic-update-slice_fusion.5 = bf16[80,2,640,320]{3,2,1,0:T(8,128)(2,1)} fusion(bf16[80,2,640,320]{3,2,1,0:T(8,128)(2,1)} %constant_dynamic-update-slice_fusion.6, bf16[80,2,80,320]{3,2,1,0:T(8,128)(2,1)} %copy-done.2), kind=kLoop, calls=%fused_computation.418 | loop fusion | bytes 19660800
  671.6 8.5 constant_dynamic-update-slice_fusion.4
  680.0 8.5 constant_dynamic-update-slice_fusion.3
  688.5 8.6 %constant_dynamic-update-slice_fusion.2 = bf16[80,2,640,320]{3,2,1,0:T(8,128)(2,1)} fusion(bf16[80,2,640,320]{3,2,1,0:T(8,128)(2,1)} %constant_dynamic-update-slice_fusion.3, bf16[80,2,80,320]{3,2,1,0:T(8,128)(2,1)} %collective-permute-done.1), kind=kLoop, calls=%fused_computation.415 | loop fusion | bytes 19660800
  697.1 8.5 %constant_dynamic-update-slice_fusion.1 = bf16[80,2,640,320]{3,2,1,0:T(8,128)(2,1)} fusion(bf16[80,2,640,320]{3,2,1,0:T(8,128)(2,1)} %constant_dynamic-update-slice_fusion.2, bf16[80,2,80,320]{3,2,1,0:T(8,128)(2,1)} %copy-done.2), kind=kLoop, calls=%fused_computation.414 | loop fusion | bytes 19660800
  705.6 8.5 %constant_dynamic-update-slice_fusion = bf16[80,2,640,320]{3,2,1,0:T(8,128)(2,1)} fusion(bf16[80,2,640,320]{3,2,1,0:T(8,128)(2,1)} %constant_dynamic-update-slice_fusion.1, bf16[80,2,80,320]{3,2,1,0:T(8,128)(2,1)} %param.12), kind=kLoop, calls=%fused_computation.413 | loop fusion | bytes 19660800 | tf_op jit(solution)/shard_map/jit(_roll_dynamic)/concatenate | solution.py:101
  714.1 17.4 %fusion.2 = f32[80,2,320,2,2]{2,4,3,1,0:T(2,128)S(1)} fusion(bf16[80,2,640,320]{3,2,1,0:T(8,128)(2,1)} %constant_dynamic-update-slice_fusion, s32[]{:T(128)S(6)} %select_n.55, bf16[80,1,2,2,320]{4,3,2,1,0:T(2,128)(2,1)S(1)} %fusion.203, bf16[80,1,2,2,320]{4,3,2,1,0:T(2,128)(2,1)S(1)} %get-tuple-element.2), kind=kOutput, calls=%fused_computation.2 | convolution fusion | flops 131891200 | bytes 40550404 | tf_op jit(solution)/shard_map/rpij,rpclj->rpicl/dot_general | solution.py:104
  738.3 28.1 %all-to-all-done.1 = f32[80,2,320,2,2]{0,4,3,1,2:T(2,128)S(1)} async-done(((f32[80,2,320,2,2]{0,4,3,1,2:T(2,128)}), f32[80,2,320,2,2]{0,4,3,1,2:T(2,128)S(1)}, u32[]{:S(2)}, u32[]{:S(2)}) %all-to-all-start.1) | async-done | bytes 819232 | tf_op jit(solution)/shard_map/all_to_all | solution.py:107
  773.1 19.5 %all_to_all.72 = bf16[80,2,80,2,8]{2,3,1,0,4:T(2,128)(2,1)S(1)} all-to-all(bf16[80,2,80,2,8]{2,3,1,0,4:T(2,128)(2,1)S(1)} %copy.62), channel_id=1, replica_groups=mesh['lat'=8,'lev'=4] {'lev'}, dimensions={4} | all-to-all | bytes 819200 | tf_op jit(solution)/shard_map/all_to_all | solution.py:110
  794.7 16.7 %fusion.23 = f32[2,80,2,2,320]{4,0,3,2,1:T(2,128)S(1)} fusion(bf16[80,2,320,2,2]{2,4,3,1,0:T(2,128)(2,1)S(1)} %all_to_all.63, bf16[80,2,640,320]{3,2,1,0:T(8,128)(2,1)} %constant_dynamic-update-slice_fusion, s32[]{:T(128)S(6)} %select_n.55), kind=kOutput, calls=%fused_computation.72 | convolution fusion | flops 131072000 | bytes 40550404 | tf_op jit(solution)/shard_map/rpij,rpicl->lrpcj/dot_general | solution.py:111
  821.3 16.1 %cosine_multiply_fusion = (f32[640,1,1280]{2,0,1:T(8,128)}, f32[640,1,1280]{2,0,1:T(8,128)}) fusion(f32[640]{0:T(1024)S(1)} %select_multiply_fusion, s32[640]{0:T(1024)S(1)} %copy-done.5), kind=kLoop, calls=%fused_computation.59 | loop fusion | flops 9830400 | bytes 6558720 | tf_op jit(solution)/shard_map/mul | solution.py:57
  840.5 7.7 fusion.22
  (80 shorter events, 88.6 us)
Async XLA Ops:
  0.6 769.7 %copy-start = (f32[8,8]{1,0:T(8,128)S(1)}, f32[8,8]{1,0:T(8,128)}, u32[]{:S(2)}) copy-start(f32[8,8]{1,0:T(8,128)} %param.14) | copy-start | bytes 772
  0.6 237.3 %copy-start.3 = (s32[2,80,1280]{2,1,0:T(8,128)S(1)}, s32[2,80,1280]{2,1,0:T(8,128)}, u32[]{:S(2)}) copy-start(s32[2,80,1280]{2,1,0:T(8,128)} %param.9) | copy-start | bytes 2457604
  0.7 216.7 %collective-permute-start = (bf16[80,2,80,320]{3,2,1,0:T(8,128)(2,1)}, bf16[80,2,80,320]{3,2,1,0:T(8,128)(2,1)S(1)}, u32[]{:S(2)}, u32[]{:S(2)}) collective-permute-start(bf16[80,2,80,320]{3,2,1,0:T(8,128)(2,1)} %param.12), channel_id=1, source_target_pairs={{0,1},{1,2},{2,3},{3,0},{4,5},{5,6},{6,7},{7,4},{8,9},{9,10},{10,1... | collective-permute-start | bytes 24576008 | tf_op jit(solution)/shard_map/ppermute | solution.py:100
  217.4 45.8 %copy-start.2 = (bf16[80,2,80,320]{3,2,1,0:T(8,128)(2,1)}, bf16[80,2,80,320]{3,2,1,0:T(8,128)(2,1)S(1)}, u32[]{:S(2)}) copy-start(bf16[80,2,80,320]{3,2,1,0:T(8,128)(2,1)S(1)} %collective-permute-done) | copy-start | bytes 24576004
  217.4 214.4 %collective-permute-start.1 = (bf16[80,2,80,320]{3,2,1,0:T(8,128)(2,1)S(1)}, bf16[80,2,80,320]{3,2,1,0:T(8,128)(2,1)}, u32[]{:S(2)}, u32[]{:S(2)}) collective-permute-start(bf16[80,2,80,320]{3,2,1,0:T(8,128)(2,1)S(1)} %collective-permute-done), channel_id=1, source_target_pairs={{0,1},{1,2},{2,3},{3,0},{4,5},{5,6},{6,7},{7,4},{8,9},{9,10},{10,1... | collective-permute-start | bytes 24576008 | tf_op jit(solution)/shard_map/ppermute | solution.py:100
  218.5 67.9 %collective-permute-start.4 = (f32[2,3,1280]{2,1,0:T(4,128)S(1)}, f32[2,3,1280]{2,1,0:T(4,128)S(1)}, u32[]{:S(2)}, u32[]{:S(2)}) collective-permute-start(f32[2,3,1280]{2,1,0:T(4,128)S(1)} %get-tuple-element.141), channel_id=1, source_target_pairs={{4,0},{8,4},{12,8},{16,12},{20,16},{24,20},{28,24},{5,1},{9,5},{13... | collective-permute-start | bytes 92168 | tf_op jit(solution)/shard_map/ppermute | solution.py:21
  219.8 68.4 %collective-permute-start.3 = (f32[2,3,1280]{2,1,0:T(4,128)S(1)}, f32[2,3,1280]{2,1,0:T(4,128)S(1)}, u32[]{:S(2)}, u32[]{:S(2)}) collective-permute-start(f32[2,3,1280]{2,1,0:T(4,128)S(1)} %get-tuple-element.140), channel_id=1, source_target_pairs={{0,4},{4,8},{8,12},{12,16},{16,20},{20,24},{24,28},{1,5},{5,9},{9,... | collective-permute-start | bytes 92168 | tf_op jit(solution)/shard_map/ppermute | solution.py:19
  263.2 9.7 %copy-start.5 = (s32[640]{0:T(1024)S(1)}, s32[640]{0:T(1024)}, u32[]{:S(2)}) copy-start(s32[640]{0:T(1024)} %param.11) | copy-start | bytes 7684
  272.9 13.4 %copy-start.1 = (f32[2,80,1280]{2,1,0:T(8,128)S(1)}, f32[2,80,1280]{2,1,0:T(8,128)}, u32[]{:S(2)}) copy-start(f32[2,80,1280]{2,1,0:T(8,128)} %param.8) | copy-start | bytes 2457604
  431.8 214.1 %collective-permute-start.2 = (bf16[80,2,80,320]{3,2,1,0:T(8,128)(2,1)}, bf16[80,2,80,320]{3,2,1,0:T(8,128)(2,1)}, u32[]{:S(2)}, u32[]{:S(2)}) collective-permute-start(bf16[80,2,80,320]{3,2,1,0:T(8,128)(2,1)} %collective-permute-done.1), channel_id=1, source_target_pairs={{0,1},{1,2},{2,3},{3,0},{4,5},{5,6},{6,7},{7,4},{8,9},{9,10},{10,1... | collective-permute-start | bytes 24576008 | tf_op jit(solution)/shard_map/ppermute | solution.py:100
  485.4 21.9 %all-to-all-start = ((f32[640,2,2,80]{3,2,1,0:T(2,128)}), f32[640,2,2,80]{3,2,1,0:T(2,128)S(1)}, u32[]{:S(2)}, u32[]{:S(2)}) async-start(f32[640,2,2,80]{3,2,1,0:T(2,128)} %copy.54), calls=%async_computation | async-start | bytes 2621440 | tf_op jit(solution)/shard_map/all_to_all | solution.py:93
  731.5 5.9 copy-start.6
  733.6 32.8 %all-to-all-start.1 = ((f32[80,2,320,2,2]{0,4,3,1,2:T(2,128)}), f32[80,2,320,2,2]{0,4,3,1,2:T(2,128)S(1)}, u32[]{:S(2)}, u32[]{:S(2)}) async-start(f32[80,2,320,2,2]{0,4,3,1,2:T(2,128)} %copy.57), calls=%async_computation.1 | async-start | bytes 2621440 | tf_op jit(solution)/shard_map/all_to_all | solution.py:107
  767.6 1.1 copy-start.4
  767.6 1.1 copy-start.7
  817.4 22.0 %all-to-all-start.3 = ((f32[2,80,2,640]{1,2,0,3:T(2,128)}), f32[2,80,2,640]{1,2,0,3:T(2,128)S(1)}, u32[]{:S(2)}, u32[]{:S(2)}) async-start(f32[2,80,2,640]{1,2,0,3:T(2,128)} %copy.67), calls=%async_computation.3 | async-start | bytes 2621440 | tf_op jit(solution)/shard_map/all_to_all | solution.py:117
